TPU v7x, 32 devices: a whole 2x2x4 slice. The times are simulated.
32 devices in a mesh: rows: 4 (over z), cent: 8 (over y, x, core).
Axes of the slice: x: 2, y: 2, z: 4, core: 2. Of those that a mesh axis runs over, the one named last changes fastest.
Arguments:
- train_rows: float32 [16384, 64], P('rows'), may hold values from -6 to 6
- centre_index: int32 [16384], P('cent'), may hold values from 0 to 16383
- precond: bfloat16 [16384, 16384], P('cent', 'rows'), as said below
- coefficients: float32 [16384, 128], P(('rows', 'cent')), may hold values from -6 to 6
- residual: float32 [16384, 128], P(('rows', 'cent')), may hold values from -6 to 6
- direction: float32 [16384, 128], P(('rows', 'cent')), may hold values from -6 to 6
Outputs:
- coef_next: float32 [16384, 128], P(('rows', 'cent'))
- residual_next: float32 [16384, 128], P(('rows', 'cent'))
- direction_next: float32 [16384, 128], P(('rows', 'cent'))
Inputs may be any that keep to these rules, and one draw needn't show every extreme that they name: precond is zero below its diagonal.
All inputs are finite; a program needn't handle non-finite values.
Results may differ from a plain program's by a relative error of at most 0.0047.
Values may be sent and summed in bfloat16 or wider, within the bound.
A program may use at most 128 MiB of HBM per device.

v0:
```python
import math
import jax
import jax.numpy as jnp
from jax import lax
from jax.sharding import PartitionSpec as P

FEAT = 64
OUTS = 128
ridge_weight = 0.1


def kernel_tile(block_rows, centres):
    row_sq = jnp.sum(block_rows * block_rows, axis=1)
    cen_sq = jnp.sum(centres * centres, axis=1)
    cross = jnp.dot(
        block_rows, centres.T, precision=lax.Precision.HIGHEST, preferred_element_type=jnp.float32
    )
    distance = row_sq[:, None] + cen_sq[None, :] - 2.0 * cross
    return jnp.exp(-(2.0 / FEAT) * distance).astype(jnp.bfloat16)


def kernel_pass(local_rows, centres, coef_field, combine):
    count_rows = local_rows.shape[0]
    block_size = math.gcd(count_rows, 1024)
    block_count = count_rows // block_size
    groups = local_rows.reshape(block_count, block_size, FEAT)
    tiles = lax.map(lambda group_rows: kernel_tile(group_rows, centres), groups)
    fitted_part = jnp.einsum(
        "kbc,cd->kbd", tiles, coef_field, preferred_element_type=jnp.float32
    ).reshape(count_rows, OUTS)
    fitted = combine(fitted_part)
    fitted_groups = fitted.reshape(block_count, block_size, OUTS)
    grad_part = jnp.einsum("kbc,kbd->cd", tiles, fitted_groups, preferred_element_type=jnp.float32)
    return grad_part


def on_device(train_rows, centre_index, precond, coefficients, residual, direction):
    rows_here = train_rows.shape[0]
    start_row = lax.axis_index("rows") * rows_here
    offset = centre_index - start_row
    inside = ((offset >= 0) & (offset < rows_here)).astype(jnp.float32)
    picked = train_rows[jnp.clip(offset, 0, rows_here - 1)] * inside[:, None]
    centres = lax.psum(picked, "rows")
    dir_low = direction.astype(jnp.bfloat16)
    columns = precond
    partial_field = jnp.dot(
        columns,
        lax.all_gather(dir_low, "cent", axis=0, tiled=True),
        preferred_element_type=jnp.float32,
    )
    coef_field = lax.psum(partial_field, "rows").astype(jnp.bfloat16)

    def line_sum(part):
        return lax.psum(part, "cent").astype(jnp.bfloat16)

    grad_part = kernel_pass(train_rows, centres, coef_field, line_sum)
    grad = lax.psum(grad_part, "rows")
    grad_low = (grad * float(rows_here * lax.axis_size("rows")) ** (-0.5)).astype(jnp.bfloat16)
    columns = precond
    image = lax.psum_scatter(
        lax.dot_general(
            columns, grad_low, (((0,), (0,)), ((), ())), preferred_element_type=jnp.float32
        ),
        "cent",
        scatter_dimension=0,
        tiled=True,
    )
    image = image + ridge_weight * direction
    norm_old, curvature = lax.psum(
        (jnp.sum(residual * residual), jnp.sum(direction * image)), ("rows", "cent")
    )
    step_size = norm_old / curvature
    coef_next = coefficients + step_size * direction
    residual_next = residual - step_size * image
    norm_new = lax.psum(jnp.sum(residual_next * residual_next), ("rows", "cent"))
    direction_next = residual_next + norm_new / norm_old * direction
    return (coef_next, residual_next, direction_next)


def solution(mesh):
    placed = (
        P("rows", None),
        P("cent"),
        P("cent", "rows"),
        P(("rows", "cent"), None),
        P(("rows", "cent"), None),
        P(("rows", "cent"), None),
    )
    return jax.shard_map(
        on_device,
        mesh=mesh,
        in_specs=placed,
        out_specs=(P(("rows", "cent"), None), P(("rows", "cent"), None), P(("rows", "cent"), None)),
        check_vma=False,
    )
```

profile of v0, /device:TPU:0, one launch (start us, length us, event | category | flops | bytes accessed | tf_op | source)
XLA Modules:
  0.0 441.2 jit_solution(3471181950002680406)
XLA Ops:
  9.5 1.8 copy.9
  11.3 5.5 %gather_fusion = f32[2048,64]{1,0:T(8,128)S(1)} fusion(f32[4096,64]{1,0:T(8,128)S(1)} %copy.9, s32[2048]{0:T(1024)S(1)} %fusion.8), kind=kCustom, calls=%fused_computation | custom fusion | bytes 1056768 | tf_op jit(solution)/shard_map/gather | solution.py:42
  16.8 1.3 broadcast_multiply_fusion
  18.2 1.6 convert_element_type.21
  19.9 53.0 %all-reduce.6.cloned.1.call-done = f32[2048,64]{1,0:T(8,128)} async-done(((f32[2048,64]{1,0:T(8,128)}), f32[2048,64]{1,0:T(8,128)}) %all-reduce.6.cloned.1.call-update) | async-done | bytes 524304 | tf_op jit(solution)/shard_map/psum | solution.py:43
  72.9 1.6 multiply_reduce_fusion
  74.5 45.0 %while.12 = (s32[]{:T(128)}, bf16[4,1024,2048]{2,1,0:T(8,128)(2,1)}, f32[4,1024,64]{2,1,0:T(8,128)S(1)}, f32[2048]{0:T(1024)S(1)}, f32[2048,64]{1,0:T(8,128)}, /*index=5*/s32[]{:T(128)}) while((s32[]{:T(128)}, bf16[4,1024,2048]{2,1,0:T(8,128)(2,1)}, f32[4,1024,64]{2,1,0:T(8,128)S(1)}, f32[2048]{0:T(1024)S(1)}, f32[2048,64]{1,0:T(8,128)}, ...), condition=%wide.region_6.7_spmd, body=%wide.region_4.0_spmd.sunk | while | flops 1621228544 | bytes 6046793 | solution.py:27
  74.7 11.0 %bitcast_dynamic-update-slice_fusion.2 = bf16[4,1024,2048]{2,1,0:T(8,128)(2,1)} fusion(bf16[4,1024,2048]{2,1,0:T(8,128)(2,1)} %get-tuple-element.116, s32[]{:T(128)} %get-tuple-element.115, f32[2048,64]{1,0:T(8,128)} %get-tuple-element.125, f32[2048]{0:T(1024)S(1)} %get-tuple-element.124, f32[1024]{0:T(1024)S(1)} %fusion.23, ...), kind=kOutput, calls=%fused_computation.2.clone.1 | convolution fusion | flops 1621098496 | bytes 5780480 | tf_op jit(solution)/shard_map/while/body/eval_jaxpr/dot_general | solution.py:15
  85.9 11.1 %bitcast_dynamic-update-slice_fusion.2 = bf16[4,1024,2048]{2,1,0:T(8,128)(2,1)} fusion(bf16[4,1024,2048]{2,1,0:T(8,128)(2,1)} %get-tuple-element.116, s32[]{:T(128)} %get-tuple-element.115, f32[2048,64]{1,0:T(8,128)} %get-tuple-element.125, f32[2048]{0:T(1024)S(1)} %get-tuple-element.124, f32[1024]{0:T(1024)S(1)} %fusion.23, ...), kind=kOutput, calls=%fused_computation.2.clone.1 | convolution fusion | flops 1621098496 | bytes 5780480 | tf_op jit(solution)/shard_map/while/body/eval_jaxpr/dot_general | solution.py:15
  97.2 11.0 %bitcast_dynamic-update-slice_fusion.2 = bf16[4,1024,2048]{2,1,0:T(8,128)(2,1)} fusion(bf16[4,1024,2048]{2,1,0:T(8,128)(2,1)} %get-tuple-element.116, s32[]{:T(128)} %get-tuple-element.115, f32[2048,64]{1,0:T(8,128)} %get-tuple-element.125, f32[2048]{0:T(1024)S(1)} %get-tuple-element.124, f32[1024]{0:T(1024)S(1)} %fusion.23, ...), kind=kOutput, calls=%fused_computation.2.clone.1 | convolution fusion | flops 1621098496 | bytes 5780480 | tf_op jit(solution)/shard_map/while/body/eval_jaxpr/dot_general | solution.py:15
  108.4 11.1 %bitcast_dynamic-update-slice_fusion.2 = bf16[4,1024,2048]{2,1,0:T(8,128)(2,1)} fusion(bf16[4,1024,2048]{2,1,0:T(8,128)(2,1)} %get-tuple-element.116, s32[]{:T(128)} %get-tuple-element.115, f32[2048,64]{1,0:T(8,128)} %get-tuple-element.125, f32[2048]{0:T(1024)S(1)} %get-tuple-element.124, f32[1024]{0:T(1024)S(1)} %fusion.23, ...), kind=kOutput, calls=%fused_computation.2.clone.1 | convolution fusion | flops 1621098496 | bytes 5780480 | tf_op jit(solution)/shard_map/while/body/eval_jaxpr/dot_general | solution.py:15
  119.5 8.4 %fusion.10 = f32[2048,128]{1,0:T(8,128)S(1)} fusion(bf16[2048,4096]{1,0:T(8,128)(2,1)} %param.10, bf16[4096,128]{1,0:T(8,128)(2,1)} %all-gather.2.cloned.1.call-done), kind=kOutput, calls=%fused_computation.28 | convolution fusion | flops 2147483648 | bytes 18874368 | tf_op jit(solution)/shard_map/dot_general | solution.py:46
  127.9 41.5 %all-reduce.9 = bf16[2048,128]{1,0:T(8,128)(2,1)S(1)} all-reduce(f32[2048,128]{1,0:T(8,128)S(1)} %fusion.10), channel_id=1, replica_groups=mesh['rows'=4,'cent'=8] {'rows'}, use_global_device_ids=true, to_apply=%region_7.8 | all-reduce | flops 262144 | bytes 1572864 | tf_op jit(solution)/shard_map/psum | solution.py:51
  169.5 8.2 %fusion.4 = f32[4,1024,128]{2,1,0:T(8,128)S(1)} fusion(bf16[4,1024,2048]{2,1,0:T(8,128)(2,1)} %get-tuple-element.58, bf16[2048,128]{1,0:T(8,128)(2,1)S(1)} %all-reduce.9), kind=kOutput, calls=%fused_computation.12 | convolution fusion | flops 2147483648 | bytes 19398656 | tf_op jit(solution)/shard_map/kbc,cd->kbd/dot_general | solution.py:28
  177.6 56.6 %all-reduce.10 = bf16[4096,128]{1,0:T(8,128)(2,1)S(1)} all-reduce(f32[4096,128]{1,0:T(8,128)S(1)} %bitcast.34), channel_id=1, replica_groups=mesh['rows'=4,'cent'=8] {'cent'}, use_global_device_ids=true, to_apply=%region_8.9 | all-reduce | flops 524288 | bytes 3145728 | tf_op jit(solution)/shard_map/psum | solution.py:54
  234.2 9.2 %convolution_bitcast_fusion.1 = f32[2048,128]{1,0:T(8,128)} fusion(bf16[4,1024,2048]{2,1,0:T(8,128)(2,1)} %get-tuple-element.58, bf16[4,1024,128]{2,1,0:T(8,128)(2,1)S(1)} %bitcast.35), kind=kOutput, calls=%fused_computation.9 | convolution fusion | flops 2147483648 | bytes 18874368 | tf_op jit(solution)/shard_map/kbc,kbd->cd/dot_general | solution.py:33
  243.5 50.6 %all-reduce.8.cloned.1.call-done = f32[2048,128]{1,0:T(8,128)} async-done(((f32[2048,128]{1,0:T(8,128)}), f32[2048,128]{1,0:T(8,128)}) %all-reduce.8.cloned.1.call-update) | async-done | bytes 1048592 | tf_op jit(solution)/shard_map/psum | solution.py:57
  294.0 9.8 %convolution_bitcast_fusion = f32[4096,128]{0,1:T(8,128)} fusion(bf16[2048,4096]{1,0:T(8,128)(2,1)} %param.10, f32[2048,128]{1,0:T(8,128)} %all-reduce.8.cloned.1.call-done), kind=kOutput, calls=%fused_computation.8 | convolution fusion | flops 2148007936 | bytes 19922944 | tf_op jit(solution)/shard_map/dot_general | solution.py:61
  304.8 39.4 %reduce-scatter.2.cloned.1.call-done = f32[512,128]{0,1:T(8,128)} async-done(((f32[4096,128]{0,1:T(8,128)}), f32[512,128]{0,1:T(8,128)}) %reduce-scatter.2.cloned.1.call-update) | async-done | bytes 262160 | tf_op jit(solution)/shard_map/reduce_scatter | solution.py:60
  344.2 1.6 multiply_reduce_fusion.2
  346.0 39.6 %all-reduce = (f32[]{:T(128)}, f32[]{:T(128)}) all-reduce(f32[]{:T(128)} %multiply_reduce_fusion.3, f32[]{:T(128)} %multiply_reduce_fusion.2), channel_id=1, replica_groups=mesh['rows'=4,'cent'=8] {'rows','cent'}, use_global_device_ids=true, to_apply=%region_1.2 | all-reduce | flops 2 | bytes 16 | tf_op jit(solution)/shard_map/psum | solution.py:69
  386.9 1.6 multiply_reduce_fusion.1
  388.6 41.3 %psum.55 = f32[]{:T(128)} all-reduce(f32[]{:T(128)} %get-tuple-element.74), channel_id=1, replica_groups=mesh['rows'=4,'cent'=8] {'rows','cent'}, use_global_device_ids=true, to_apply=%region_14.15 | all-reduce | flops 1 | bytes 8 | tf_op jit(solution)/shard_map/psum | solution.py:75
  432.1 0.8 copy.17
  (29 shorter events, 5.3 us)
Async XLA Ops:
  8.0 64.9 %all-reduce.6.cloned.1.call-start = ((), (), s32[]{:S(2)}) async-start(), calls=%async_computation.1 | async-start | bytes 2097152 | tf_op jit(solution)/shard_map/psum | solution.py:43
  18.1 101.4 %all-gather.2.cloned.1.call-start = ((), (), s32[]{:S(2)}) async-start(), calls=%async_computation.2 | async-start | bytes 1179648 | tf_op jit(solution)/shard_map/all_gather | solution.py:48
  19.8 274.2 %all-reduce.8.cloned.1.call-start = ((), (), s32[]{:S(2)}) async-start(), calls=%async_computation.3 | async-start | bytes 2097152 | tf_op jit(solution)/shard_map/psum | solution.py:57
  243.4 60.5 %copy-start = (f32[512,128]{1,0:T(8,128)S(1)}, f32[512,128]{1,0:T(8,128)}, u32[]{:S(2)}) copy-start(f32[512,128]{1,0:T(8,128)} %param.13) | copy-start | bytes 786436
  243.4 60.7 %copy-start.1 = (f32[512,128]{1,0:T(8,128)S(1)}, f32[512,128]{1,0:T(8,128)}, u32[]{:S(2)}) copy-start(f32[512,128]{1,0:T(8,128)} %param.12) | copy-start | bytes 786436
  243.4 102.5 %copy-start.2 = (f32[512,128]{1,0:T(8,128)S(1)}, f32[512,128]{1,0:T(8,128)}, u32[]{:S(2)}) copy-start(f32[512,128]{1,0:T(8,128)} %param.11) | copy-start | bytes 786436
  243.4 100.8 %reduce-scatter.2.cloned.1.call-start = ((), (), s32[]{:S(2)}) async-start(), calls=%async_computation.4 | async-start | bytes 2359296 | tf_op jit(solution)/shard_map/reduce_scatter | solution.py:60
Sparse Core Ops, SparseCore 0:
  18.2 54.6 all-reduce.5
  243.5 50.4 all-reduce.7
Sparse Core Ops, SparseCore 1:
  21.1 25.9 all-gather.1
  304.0 40.2 reduce-scatter.1
where the time goes:
time: 442 us; the launch traced here: 441 us
  blocking collectives  179 us (40%)
  waiting for transfers between devices  143 us (32%)
  matrix products  79.7 us (18%)
  between operations  18.3 us (4%)
  other arithmetic  10.7 us (2%)
  local copies, waits for them, and re-layouts  10.2 us (2%)
    psum x1, blocking collectives, line_sum(): return lax.psum(part, 'cent').astype(jnp.bfloat16)  56.6 us
    psum x1, waiting for transfers between devices, on_device(): centres = lax.psum(picked, 'rows')  53 us
    psum x1, waiting for transfers between devices, on_device(): grad = lax.psum(grad_part, 'rows')  50.6 us
    dot_general x4, matrix products, kernel_tile(): jnp.dot(block_rows, centres.T, precision=lax.Precision.HIGHEST, preferred...  44.2 us
    psum x1, blocking collectives, on_device(): coef_field = lax.psum(partial_field, 'rows').astype(jnp.bfloat16)  41.5 us
    psum x1, blocking collectives, on_device(): lax.psum(jnp.sum(residual_next * residual_next), ('rows', 'cent'))  41.3 us
    psum x1, blocking collectives, on_device(): lax.psum((jnp.sum(residual * residual), jnp.sum(direction * image)), ('ro...  39.6 us
    reduce_scatter x1, waiting for transfers between devices, on_device(): lax.psum_scatter(lax.dot_general(columns, grad_low, (((0,), (0,)), ((), (...  39.4 us
  transfers between devices with their start and end apart: 4, of which 3 were waited for; matrix products, arithmetic and copies ran while one was open for 11% of the time, Pallas kernels for 0%

commit v1 on v0

--- a/solution.py
+++ b/solution.py
@@ -54,7 +54,9 @@
         return lax.psum(part, "cent").astype(jnp.bfloat16)
 
     grad_part = kernel_pass(train_rows, centres, coef_field, line_sum)
-    grad = lax.psum(grad_part, "rows")
+    grad = grad_part
+    for hop in (1, 2):
+        grad = grad + lax.ppermute(grad, "rows", [(dev, dev ^ hop) for dev in range(4)])
     grad_low = (grad * float(rows_here * lax.axis_size("rows")) ** (-0.5)).astype(jnp.bfloat16)
     columns = precond
     image = lax.psum_scatter(

time: 442 us -> 461 us (1.043)
  waiting for transfers between devices: 143 us -> 160 us
    ppermute x0 -> x2, waiting for transfers between devices: none -> 65.5 us  [on_device(): lax.ppermute(grad, 'rows', [(dev, dev ^ hop) for dev in range(4)])]
    psum x1 -> x0, waiting for transfers between devices: 50.6 us -> none  [on_device(): grad = lax.psum(grad_part, 'rows')]
  transfers between devices with their start and end apart: 4 -> 5, of which waited for: 3 -> 4; matrix products, arithmetic and copies ran while one was open for 11% -> 11% of each run, Pallas kernels for 0% -> 0%
where the time goes in v1:
time: 461 us; the launch traced here: 460 us
  blocking collectives  179 us (39%)
  waiting for transfers between devices  160 us (35%)
  matrix products  78.5 us (17%)
  between operations  18.3 us (4%)
  other arithmetic  10.8 us (2%)
  local copies, waits for them, and re-layouts  10.2 us (2%)
    ppermute x2, waiting for transfers between devices, on_device(): lax.ppermute(grad, 'rows', [(dev, dev ^ hop) for dev in range(4)])  65.5 us
    psum x1, blocking collectives, line_sum(): return lax.psum(part, 'cent').astype(jnp.bfloat16)  56.6 us
    psum x1, waiting for transfers between devices, on_device(): centres = lax.psum(picked, 'rows')  53 us
    dot_general x4, matrix products, kernel_tile(): jnp.dot(block_rows, centres.T, precision=lax.Precision.HIGHEST, preferred...  44.2 us
    reduce_scatter x1, waiting for transfers between devices, on_device(): lax.psum_scatter(lax.dot_general(columns, grad_low, (((0,), (0,)), ((), (...  41.7 us
    psum x1, blocking collectives, on_device(): coef_field = lax.psum(partial_field, 'rows').astype(jnp.bfloat16)  41.5 us
    psum x1, blocking collectives, on_device(): lax.psum(jnp.sum(residual_next * residual_next), ('rows', 'cent'))  41.3 us
    psum x1, blocking collectives, on_device(): lax.psum((jnp.sum(residual * residual), jnp.sum(direction * image)), ('ro...  39.6 us
  transfers between devices with their start and end apart: 5, of which 4 were waited for; matrix products, arithmetic and copies ran while one was open for 11% of the time, Pallas kernels for 0%

profile of v1, /device:TPU:0, one launch (start us, length us, event | category | flops | bytes accessed | tf_op | source)
XLA Modules:
  0.0 460.3 jit_solution(7665831548889880813)
XLA Ops:
  9.5 1.8 copy.9
  11.3 5.5 %gather_fusion = f32[2048,64]{1,0:T(8,128)S(1)} fusion(f32[4096,64]{1,0:T(8,128)S(1)} %copy.9, s32[2048]{0:T(1024)S(1)} %fusion.8), kind=kCustom, calls=%fused_computation | custom fusion | bytes 1056768 | tf_op jit(solution)/shard_map/gather | solution.py:42
  18.2 1.6 convert_element_type.21
  19.9 53.0 %all-reduce.5.cloned.1.call-done = f32[2048,64]{1,0:T(8,128)} async-done(((f32[2048,64]{1,0:T(8,128)}), f32[2048,64]{1,0:T(8,128)}) %all-reduce.5.cloned.1.call-update) | async-done | bytes 524304 | tf_op jit(solution)/shard_map/psum | solution.py:43
  72.9 1.6 multiply_reduce_fusion
  74.5 45.0 %while.12 = (s32[]{:T(128)}, bf16[4,1024,2048]{2,1,0:T(8,128)(2,1)}, f32[4,1024,64]{2,1,0:T(8,128)S(1)}, f32[2048]{0:T(1024)S(1)}, f32[2048,64]{1,0:T(8,128)}, /*index=5*/s32[]{:T(128)}) while((s32[]{:T(128)}, bf16[4,1024,2048]{2,1,0:T(8,128)(2,1)}, f32[4,1024,64]{2,1,0:T(8,128)S(1)}, f32[2048]{0:T(1024)S(1)}, f32[2048,64]{1,0:T(8,128)}, ...), condition=%wide.region_6.7_spmd, body=%wide.region_4.0_spmd.sunk | while | flops 1621228544 | bytes 6046793 | solution.py:27
  74.7 11.0 %bitcast_dynamic-update-slice_fusion.2 = bf16[4,1024,2048]{2,1,0:T(8,128)(2,1)} fusion(bf16[4,1024,2048]{2,1,0:T(8,128)(2,1)} %get-tuple-element.116, s32[]{:T(128)} %get-tuple-element.115, f32[2048,64]{1,0:T(8,128)} %get-tuple-element.125, f32[2048]{0:T(1024)S(1)} %get-tuple-element.124, f32[1024]{0:T(1024)S(1)} %fusion.23, ...), kind=kOutput, calls=%fused_computation.2.clone.1 | convolution fusion | flops 1621098496 | bytes 5780480 | tf_op jit(solution)/shard_map/while/body/eval_jaxpr/dot_general | solution.py:15
  85.9 11.1 %bitcast_dynamic-update-slice_fusion.2 = bf16[4,1024,2048]{2,1,0:T(8,128)(2,1)} fusion(bf16[4,1024,2048]{2,1,0:T(8,128)(2,1)} %get-tuple-element.116, s32[]{:T(128)} %get-tuple-element.115, f32[2048,64]{1,0:T(8,128)} %get-tuple-element.125, f32[2048]{0:T(1024)S(1)} %get-tuple-element.124, f32[1024]{0:T(1024)S(1)} %fusion.23, ...), kind=kOutput, calls=%fused_computation.2.clone.1 | convolution fusion | flops 1621098496 | bytes 5780480 | tf_op jit(solution)/shard_map/while/body/eval_jaxpr/dot_general | solution.py:15
  97.2 11.0 %bitcast_dynamic-update-slice_fusion.2 = bf16[4,1024,2048]{2,1,0:T(8,128)(2,1)} fusion(bf16[4,1024,2048]{2,1,0:T(8,128)(2,1)} %get-tuple-element.116, s32[]{:T(128)} %get-tuple-element.115, f32[2048,64]{1,0:T(8,128)} %get-tuple-element.125, f32[2048]{0:T(1024)S(1)} %get-tuple-element.124, f32[1024]{0:T(1024)S(1)} %fusion.23, ...), kind=kOutput, calls=%fused_computation.2.clone.1 | convolution fusion | flops 1621098496 | bytes 5780480 | tf_op jit(solution)/shard_map/while/body/eval_jaxpr/dot_general | solution.py:15
  108.4 11.1 %bitcast_dynamic-update-slice_fusion.2 = bf16[4,1024,2048]{2,1,0:T(8,128)(2,1)} fusion(bf16[4,1024,2048]{2,1,0:T(8,128)(2,1)} %get-tuple-element.116, s32[]{:T(128)} %get-tuple-element.115, f32[2048,64]{1,0:T(8,128)} %get-tuple-element.125, f32[2048]{0:T(1024)S(1)} %get-tuple-element.124, f32[1024]{0:T(1024)S(1)} %fusion.23, ...), kind=kOutput, calls=%fused_computation.2.clone.1 | convolution fusion | flops 1621098496 | bytes 5780480 | tf_op jit(solution)/shard_map/while/body/eval_jaxpr/dot_general | solution.py:15
  119.5 8.4 %fusion.10 = f32[2048,128]{1,0:T(8,128)S(1)} fusion(bf16[2048,4096]{1,0:T(8,128)(2,1)} %param.10, bf16[4096,128]{1,0:T(8,128)(2,1)} %all-gather.2.cloned.1.call-done), kind=kOutput, calls=%fused_computation.28 | convolution fusion | flops 2147483648 | bytes 18874368 | tf_op jit(solution)/shard_map/dot_general | solution.py:46
  127.9 41.5 %all-reduce.6 = bf16[2048,128]{1,0:T(8,128)(2,1)S(1)} all-reduce(f32[2048,128]{1,0:T(8,128)S(1)} %fusion.10), channel_id=1, replica_groups=mesh['rows'=4,'cent'=8] {'rows'}, use_global_device_ids=true, to_apply=%region_7.8 | all-reduce | flops 262144 | bytes 1572864 | tf_op jit(solution)/shard_map/psum | solution.py:51
  169.5 8.2 %fusion.4 = f32[4,1024,128]{2,1,0:T(8,128)S(1)} fusion(bf16[4,1024,2048]{2,1,0:T(8,128)(2,1)} %get-tuple-element.58, bf16[2048,128]{1,0:T(8,128)(2,1)S(1)} %all-reduce.6), kind=kOutput, calls=%fused_computation.12 | convolution fusion | flops 2147483648 | bytes 19398656 | tf_op jit(solution)/shard_map/kbc,cd->kbd/dot_general | solution.py:28
  177.6 56.6 %all-reduce.7 = bf16[4096,128]{1,0:T(8,128)(2,1)S(1)} all-reduce(f32[4096,128]{1,0:T(8,128)S(1)} %bitcast.34), channel_id=1, replica_groups=mesh['rows'=4,'cent'=8] {'cent'}, use_global_device_ids=true, to_apply=%region_8.9 | all-reduce | flops 524288 | bytes 3145728 | tf_op jit(solution)/shard_map/psum | solution.py:54
  234.3 8.1 %convolution_bitcast_fusion.1 = f32[2048,128]{1,0:T(8,128)S(1)} fusion(bf16[4,1024,2048]{2,1,0:T(8,128)(2,1)} %get-tuple-element.58, bf16[4,1024,128]{2,1,0:T(8,128)(2,1)S(1)} %bitcast.35), kind=kOutput, calls=%fused_computation.9 | convolution fusion | flops 2147483648 | bytes 18874368 | tf_op jit(solution)/shard_map/kbc,kbd->cd/dot_general | solution.py:33
  242.5 22.9 %collective-permute-done = f32[2048,128]{1,0:T(8,128)S(1)} collective-permute-done((f32[2048,128]{1,0:T(8,128)S(1)}, f32[2048,128]{1,0:T(8,128)S(1)}, u32[]{:S(2)}, u32[]{:S(2)}) %collective-permute-start) | collective-permute-done | bytes 1048608 | tf_op jit(solution)/shard_map/ppermute | solution.py:59
  265.6 2.9 collective-permute-start.1
  268.5 42.6 %collective-permute-done.1 = f32[2048,128]{1,0:T(8,128)S(1)} collective-permute-done((f32[2048,128]{1,0:T(8,128)S(1)}, f32[2048,128]{1,0:T(8,128)S(1)}, u32[]{:S(2)}, u32[]{:S(2)}) %collective-permute-start.1) | collective-permute-done | bytes 1048608 | tf_op jit(solution)/shard_map/ppermute | solution.py:59
  311.1 9.6 %convolution_bitcast_fusion = f32[4096,128]{0,1:T(8,128)} fusion(bf16[2048,4096]{1,0:T(8,128)(2,1)} %param.10, f32[2048,128]{1,0:T(8,128)S(1)} %add.57, f32[2048,128]{1,0:T(8,128)S(1)} %collective-permute-done.1), kind=kOutput, calls=%fused_computation.8 | convolution fusion | flops 2148270080 | bytes 20971520 | tf_op jit(solution)/shard_map/dot_general | solution.py:63
  321.6 41.7 %reduce-scatter.2.cloned.1.call-done = f32[512,128]{0,1:T(8,128)} async-done(((f32[4096,128]{0,1:T(8,128)}), f32[512,128]{0,1:T(8,128)}) %reduce-scatter.2.cloned.1.call-update) | async-done | bytes 262160 | tf_op jit(solution)/shard_map/reduce_scatter | solution.py:62
  363.3 1.6 multiply_reduce_fusion.2
  365.1 39.6 %all-reduce = (f32[]{:T(128)}, f32[]{:T(128)}) all-reduce(f32[]{:T(128)} %multiply_reduce_fusion.3, f32[]{:T(128)} %multiply_reduce_fusion.2), channel_id=1, replica_groups=mesh['rows'=4,'cent'=8] {'rows','cent'}, use_global_device_ids=true, to_apply=%region_1.2 | all-reduce | flops 2 | bytes 16 | tf_op jit(solution)/shard_map/psum | solution.py:71
  406.0 1.6 multiply_reduce_fusion.1
  407.7 41.3 %psum.47 = f32[]{:T(128)} all-reduce(f32[]{:T(128)} %get-tuple-element.74), channel_id=1, replica_groups=mesh['rows'=4,'cent'=8] {'rows','cent'}, use_global_device_ids=true, to_apply=%region_13.14 | all-reduce | flops 1 | bytes 8 | tf_op jit(solution)/shard_map/psum | solution.py:77
  (31 shorter events, 7.6 us)
Async XLA Ops:
  8.0 64.9 %all-reduce.5.cloned.1.call-start = ((), (), s32[]{:S(2)}) async-start(), calls=%async_computation.1 | async-start | bytes 2097152 | tf_op jit(solution)/shard_map/psum | solution.py:43
  18.1 101.4 %all-gather.2.cloned.1.call-start = ((), (), s32[]{:S(2)}) async-start(), calls=%async_computation.2 | async-start | bytes 1179648 | tf_op jit(solution)/shard_map/all_gather | solution.py:48
  19.8 343.5 %reduce-scatter.2.cloned.1.call-start = ((), (), s32[]{:S(2)}) async-start(), calls=%async_computation.3 | async-start | bytes 2359296 | tf_op jit(solution)/shard_map/reduce_scatter | solution.py:62
  242.4 78.3 %copy-start = (f32[512,128]{1,0:T(8,128)S(1)}, f32[512,128]{1,0:T(8,128)}, u32[]{:S(2)}) copy-start(f32[512,128]{1,0:T(8,128)} %param.13) | copy-start | bytes 786436
  242.4 78.4 %copy-start.1 = (f32[512,128]{1,0:T(8,128)S(1)}, f32[512,128]{1,0:T(8,128)}, u32[]{:S(2)}) copy-start(f32[512,128]{1,0:T(8,128)} %param.12) | copy-start | bytes 786436
  242.4 23.0 %collective-permute-start = (f32[2048,128]{1,0:T(8,128)S(1)}, f32[2048,128]{1,0:T(8,128)S(1)}, u32[]{:S(2)}, u32[]{:S(2)}) collective-permute-start(f32[2048,128]{1,0:T(8,128)S(1)} %convolution_bitcast_fusion.1), channel_id=1, source_target_pairs={{0,8},{8,0},{16,24},{24,16},{1,9},{9,1},{17,25},{25,17},{2,10},{10... | collective-permute-start | bytes 3145736 | tf_op jit(solution)/shard_map/ppermute | solution.py:59
  265.5 99.4 %copy-start.2 = (f32[512,128]{1,0:T(8,128)S(1)}, f32[512,128]{1,0:T(8,128)}, u32[]{:S(2)}) copy-start(f32[512,128]{1,0:T(8,128)} %param.11) | copy-start | bytes 786436
  265.6 45.5 %collective-permute-start.1 = (f32[2048,128]{1,0:T(8,128)S(1)}, f32[2048,128]{1,0:T(8,128)S(1)}, u32[]{:S(2)}, u32[]{:S(2)}) collective-permute-start(f32[2048,128]{1,0:T(8,128)S(1)} %add.57), channel_id=1, source_target_pairs={{0,16},{8,24},{16,0},{24,8},{1,17},{9,25},{17,1},{25,9},{2,18},{10... | collective-permute-start | bytes 3145736 | tf_op jit(solution)/shard_map/ppermute | solution.py:59
Sparse Core Ops, SparseCore 0:
  18.2 54.6 all-reduce.4
Sparse Core Ops, SparseCore 1:
  21.1 25.9 all-gather.1
  320.8 42.5 reduce-scatter.1
